TPU v7x, 32 devices: a whole 2x2x4 slice. The times are simulated.
32 devices in a mesh: chan: 8 (over z, y), row: 2 (over core), col: 2 (over x).
Axes of the slice: x: 2, y: 2, z: 4, core: 2. Of those that a mesh axis runs over, the one named last changes fastest.
Arguments:
- volts: bfloat16 [2, 1024, 2, 52736], P(None, ('chan', 'row', 'col')), may hold values from -6 to 6
- taps: float32 [8, 512], replicated, may hold values from -2 to 2
- owner_map: int32 [24], replicated, may hold values from 0 to 15, as said below
- assign: int32 [512], replicated, may hold values from 0 to 511, each once
Outputs:
- visibility: bfloat16 [32, 2, 1024, 1024], P(('chan', 'col'), None, 'row')
Inputs may be any that keep to these rules, and one draw needn't show every extreme that they name: `owner_map`: each owner holds 1 to 2 channels, and some owner holds exactly 2. `assign`: A permutation of the stations.
All inputs are finite; a program needn't handle non-finite values.
Results may differ from a plain program's by a relative error of at most 0.0055.
Values may be sent and summed in bfloat16 or wider, within the bound.
No kernel may reach another device: no remote copies, remote signals or barrier semaphores. Data moves between devices by JAX's collectives and lax.ppermute only.
A program may use at most 192 MiB of HBM per device.

v0:
```python
import math

import jax
import jax.numpy as jnp
from jax import lax
from jax.sharding import PartitionSpec as P

STATIONS = 512
NFFT = 512
TAPS = 8
BATCHES = 2
CAP = 2


def slot_table(owner_map, owner_count, slot_count):
    channel_count = owner_map.shape[0]
    ranking = jnp.argsort(owner_map * channel_count + jnp.arange(channel_count, dtype=jnp.int32))
    counts = jnp.sum(
        (owner_map[None, :] == jnp.arange(owner_count, dtype=jnp.int32)[:, None]).astype(jnp.int32),
        axis=1,
    )
    starts = jnp.cumsum(counts) - counts
    slot_index = jnp.arange(slot_count, dtype=jnp.int32)
    position = jnp.clip(starts[:, None] + slot_index[None, :], 0, channel_count - 1)
    channel = jnp.take(ranking, position, axis=0)
    is_live = slot_index[None, :] < counts[:, None]
    return (channel, is_live)


def shards(volts, taps, owner_map, assign):
    chan_count = lax.axis_size("chan")
    rows_count = lax.axis_size("row")
    cols_count = lax.axis_size("col")
    owner_count = chan_count * cols_count
    local_inputs = volts.shape[1]
    spec_len = volts.shape[3] // NFFT - TAPS + 1
    channel, is_live = slot_table(owner_map, owner_count, CAP)
    points = jnp.arange(NFFT, dtype=jnp.int32)
    phase = (points[:, None, None] * channel.T[None, :, :] % NFFT).astype(jnp.float32) * (
        2.0 * math.pi / NFFT
    )
    weight_live = is_live.T[None, :, :].astype(jnp.float32) / math.sqrt(NFFT)
    cosine = jnp.cos(phase) * weight_live
    sine = jnp.sin(phase) * weight_live
    table = jnp.stack(
        [jnp.stack([cosine, -sine], axis=1), jnp.stack([sine, cosine], axis=1)], axis=0
    )
    total_inputs = 2 * STATIONS
    positions = jnp.arange(total_inputs, dtype=jnp.int32)
    pick = 2 * jnp.take(assign, positions // 2, axis=0) + positions % 2
    device_of = pick // local_inputs
    within = pick % local_inputs
    chan_of = device_of // (rows_count * cols_count)
    row_of = device_of // cols_count % rows_count
    col_of = device_of % cols_count
    located = ((row_of * cols_count + col_of) * chan_count + chan_of) * local_inputs + within
    row_count = total_inputs // rows_count
    row_pick = lax.dynamic_slice_in_dim(located, lax.axis_index("row") * row_count, row_count)
    total = jnp.zeros((CAP, 2 * row_count, total_inputs), jnp.float32)
    for batch in range(BATCHES):
        signal = (
            volts[batch].astype(jnp.float32).reshape(local_inputs, 2, spec_len + TAPS - 1, NFFT)
        )
        summed = jnp.zeros((local_inputs, 2, spec_len, NFFT), jnp.float32)
        for tap_index in range(TAPS):
            summed = (
                summed
                + taps[tap_index][None, None, None, :]
                * signal[:, :, tap_index : tap_index + spec_len, :]
            )
        result = jnp.einsum("iasj,ajbkg->kgibs", summed, table, precision=lax.Precision.HIGHEST)
        turned = lax.all_to_all(
            lax.all_to_all(
                result.reshape(CAP, chan_count, cols_count, local_inputs, 2 * spec_len).astype(
                    jnp.bfloat16
                ),
                "chan",
                split_axis=1,
                concat_axis=3,
                tiled=True,
            ),
            "col",
            split_axis=2,
            concat_axis=3,
            tiled=True,
        )
        gathered = lax.all_gather(turned, "row", axis=3, tiled=True)
        flat = gathered.reshape(CAP, total_inputs, -1)
        width = flat.shape[2]
        rows = jnp.take(flat, row_pick, axis=1)
        split_rows = rows.reshape(CAP, row_count, width // (2 * spec_len), 2, spec_len)
        flipped = jnp.stack(
            [split_rows[:, :, :, 1, :], -split_rows[:, :, :, 0, :]], axis=3
        ).reshape(CAP, row_count, width)
        stacked = jnp.concatenate([rows, flipped], axis=1)
        columns = jnp.take(flat, located, axis=1)
        total = total + jnp.einsum(
            "kpx,kqx->kpq", stacked, columns, preferred_element_type=jnp.float32
        )
    scale = 1.0 / math.sqrt(2 * BATCHES * spec_len)
    return (total * scale).reshape(CAP, 2, row_count, total_inputs).astype(jnp.bfloat16)


def solution(mesh):
    placed = (P(None, ("chan", "row", "col"), None, None), P(), P(), P())
    return jax.shard_map(
        shards,
        mesh=mesh,
        in_specs=placed,
        out_specs=P(("chan", "col"), None, "row", None),
        check_vma=False,
    )
```

profile of v0, /device:TPU:0, one launch (start us, length us, event | category | flops | bytes accessed | tf_op | source)
XLA Modules:
  0.0 369.9 jit_solution(2571589468664452819)
XLA Ops:
  0.0 0.0 copy-start
  0.0 0.8 convert_reduce_fusion
  0.8 0.7 iota_add_fusion
  1.4 14.1 %slice_convert_fusion = (f32[1,32,2,52736]{3,2,1,0:T(2,128)}, f32[1,32,2,52736]{3,2,1,0:T(2,128)}) fusion(bf16[2,32,2,52736]{3,2,1,0:T(2,128)(2,1)} %param.8), kind=kLoop, calls=%fused_computation.41 | loop fusion | flops 6750208 | bytes 40501248 | tf_op jit(solution)/shard_map/convert_element_type | solution.py:62
  15.5 26.2 %reshape.362 = f32[32,2,103,512]{3,2,1,0:T(8,128)} reshape(f32[1,32,2,52736]{3,2,1,0:T(2,128)} %get-tuple-element.29) | data formatting | bytes 27000832 | tf_op jit(solution)/shard_map/convert_element_type | solution.py:62
  41.8 0.0 copy-start.1
  41.8 71.3 %fusion.119 = (f32[32,2,96,512]{3,2,1,0:T(8,128)}, f32[32,2,96,512]{3,2,1,0:T(8,128)}, f32[32,2,96,512]{3,2,1,0:T(8,128)}, f32[32,2,96,512]{3,2,1,0:T(8,128)}, f...) fusion(f32[32,2,103,512]{3,2,1,0:T(8,128)} %reshape.362), kind=kLoop, calls=%fused_computation.175 | loop fusion | bytes 201326592 | tf_op jit(solution)/shard_map/slice | solution.py:69
  113.0 0.0 copy-done.1
  113.1 0.1 copy.71
  113.2 0.1 reduce
  113.3 0.1 compare_select_fusion.1
  113.4 0.1 reshape.329
  113.5 1.6 sort.17
  115.1 0.7 gather_fusion
  115.8 0.1 reshape.328
  115.9 0.1 bitcast_select_fusion
  116.0 0.1 copy.72
  116.1 0.4 fusion.85
  116.5 35.4 %fusion.63 = bf16[2,16,32,2,96]{4,1,2,0,3:T(8,128)(2,1)S(1)} fusion(f32[32,2,96,512]{3,2,1,0:T(8,128)} %get-tuple-element.20, f32[32,2,96,512]{3,2,1,0:T(8,128)} %get-tuple-element.14, f32[32,2,96,512]{3,2,1,0:T(8,128)} %get-tuple-element.15, f32[32,2,96,512]{3,2,1,0:T(8,128)} %get-tuple-element.16, f32[32,2,96,512]{3,2,1,0:T(8,128)} %get-tuple-element.17, ...), kind=kOutput, calls=%fused_computation.66 | convolution fusion | flops 2463367168 | bytes 101335040 | tf_op jit(solution)/shard_map/iasj,ajbkg->kgibs/dot_general | solution.py:71
  151.9 0.5 copy.87
  152.5 0.3 convert_element_type.73
  152.8 0.8 copy.88
  153.7 7.3 %all-to-all-start.2 = ((bf16[2,8,2,32,192]{4,3,2,0,1:T(8,128)(2,1)}), bf16[2,8,2,32,192]{4,3,2,0,1:T(8,128)(2,1)S(1)}, u32[]{:S(2)}, u32[]{:S(2)}) async-start(bf16[2,8,2,32,192]{4,3,2,0,1:T(8,128)(2,1)} %copy.88), calls=%async_computation.2 | async-start | bytes 1048576 | tf_op jit(solution)/shard_map/all_to_all | solution.py:73
  161.0 26.2 %reshape.361 = f32[32,2,103,512]{3,2,1,0:T(8,128)} reshape(f32[1,32,2,52736]{3,2,1,0:T(2,128)} %get-tuple-element.30) | data formatting | bytes 27000832 | tf_op jit(solution)/shard_map/convert_element_type | solution.py:62
  187.2 71.3 %fusion.120 = (f32[32,2,96,512]{3,2,1,0:T(8,128)}, f32[32,2,96,512]{3,2,1,0:T(8,128)}, f32[32,2,96,512]{3,2,1,0:T(8,128)}, f32[32,2,96,512]{3,2,1,0:T(8,128)}, f...) fusion(f32[32,2,103,512]{3,2,1,0:T(8,128)} %reshape.361), kind=kLoop, calls=%fused_computation.176 | loop fusion | bytes 201326592 | tf_op jit(solution)/shard_map/slice | solution.py:69
  258.6 35.4 %fusion.60 = bf16[2,16,32,2,96]{4,1,2,0,3:T(8,128)(2,1)S(1)} fusion(f32[32,2,96,512]{3,2,1,0:T(8,128)} %get-tuple-element.28, f32[32,2,96,512]{3,2,1,0:T(8,128)} %get-tuple-element.22, f32[32,2,96,512]{3,2,1,0:T(8,128)} %get-tuple-element.23, f32[32,2,96,512]{3,2,1,0:T(8,128)} %get-tuple-element.24, f32[32,2,96,512]{3,2,1,0:T(8,128)} %get-tuple-element.25, ...), kind=kOutput, calls=%fused_computation.65 | convolution fusion | flops 2463367168 | bytes 101335040 | tf_op jit(solution)/shard_map/iasj,ajbkg->kgibs/dot_general | solution.py:71
  294.0 0.5 copy.76
  294.6 0.3 convert_element_type.68
  294.9 0.8 copy.77
  295.7 0.0 all-to-all-done.2
  295.7 6.0 %all-to-all-start = ((bf16[2,8,2,32,192]{4,3,2,0,1:T(8,128)(2,1)}), bf16[2,8,2,32,192]{4,3,2,0,1:T(8,128)(2,1)S(1)}, u32[]{:S(2)}, u32[]{:S(2)}) async-start(bf16[2,8,2,32,192]{4,3,2,0,1:T(8,128)(2,1)} %copy.77), calls=%async_computation | async-start | bytes 1048576 | tf_op jit(solution)/shard_map/all_to_all | solution.py:73
  301.8 0.0 copy-done
  301.8 6.9 %gather_fusion.1 = s32[1024]{0:T(1024)S(1)} fusion(s32[512]{0:T(512)S(1)} %copy-done, s32[1024]{0:T(1024)S(1)} %broadcast_clamp_fusion), kind=kCustom, calls=%fused_computation.5 | custom fusion | bytes 12288 | tf_op jit(solution)/shard_map/jit(_take)/gather | solution.py:50
  308.7 0.1 compare_and_fusion.1
  308.8 1.0 copy.90
  309.8 5.9 %all-to-all-done = bf16[2,8,2,32,192]{4,3,2,0,1:T(8,128)(2,1)S(1)} async-done(((bf16[2,8,2,32,192]{4,3,2,0,1:T(8,128)(2,1)}), bf16[2,8,2,32,192]{4,3,2,0,1:T(8,128)(2,1)S(1)}, u32[]{:S(2)}, u32[]{:S(2)}) %all-to-all-start) | async-done | bytes 393248 | tf_op jit(solution)/shard_map/all_to_all | solution.py:73
  315.7 3.5 all-to-all-start.3
  319.2 0.9 copy.79
  320.2 4.9 %all-to-all-done.3 = bf16[2,1,2,256,192]{3,4,1,0,2:T(8,128)(2,1)S(1)} async-done(((bf16[2,1,2,256,192]{3,4,1,0,2:T(8,128)(2,1)}), bf16[2,1,2,256,192]{3,4,1,0,2:T(8,128)(2,1)S(1)}, u32[]{:S(2)}, u32[]{:S(2)}) %all-to-all-start.3) | async-done | bytes 393248 | tf_op jit(solution)/shard_map/all_to_all | solution.py:72
  325.0 3.5 all-to-all-start.1
  328.5 0.4 copy.91
  328.9 0.3 all_to_all.55
  329.2 2.4 all_gather.7
  331.6 0.9 copy.93
  332.4 1.9 all-to-all-done.1
  334.4 0.4 copy.80
  334.8 0.3 all_to_all.49
  335.0 2.6 all_gather.6
  337.6 0.9 copy.82
  338.5 4.2 %gather_fusion.5 = bf16[1024,2,192]{2,1,0:T(2,128)(2,1)S(1)} fusion(bf16[2,1024,192]{2,0,1:T(2,128)(2,1)S(1)} %bitcast.99, s32[1024]{0:T(1024)S(1)} %fusion.113), kind=kCustom, calls=%fused_computation.3.clone | custom fusion | bytes 1576960 | tf_op jit(solution)/shard_map/jit(_take)/gather | solution.py:96
  342.7 8.5 %gather_fusion.3 = bf16[1024,2,192]{2,1,0:T(2,128)(2,1)} fusion(bf16[2,1024,192]{2,0,1:T(2,128)(2,1)S(1)} %bitcast.101, s32[1024]{0:T(1024)S(1)} %fusion.113), kind=kCustom, calls=%fused_computation.1.clone | custom fusion | bytes 1576960 | tf_op jit(solution)/shard_map/jit(_take)/gather | solution.py:96
  351.2 3.0 gather_fusion.4
  354.2 2.6 gather_fusion.2
  356.8 1.3 copy.94
  358.1 0.4 copy.83
  358.5 0.1 broadcast_select_fusion.2
  358.8 5.5 %fusion.70 = (bf16[2,1024,192]{2,0,1:T(2,128)(2,1)S(1)}, bf16[2,1024,192]{2,0,1:T(2,128)(2,1)S(1)}) fusion(bf16[1024,2,192]{2,1,0:T(2,128)(2,1)S(1)} %gather_fusion.5, pred[1024]{0:T(1024)(128)(4,1)S(1)} %get-tuple-element.11, bf16[1024,2,192]{2,1,0:T(2,128)(2,1)} %gather_fusion.3), kind=kLoop, calls=%fused_computation.71 | loop fusion | flops 786432 | bytes 3146752 | tf_op jit(solution)/shard_map/jit(_take)/select_n | solution.py:96
  364.3 1.6 fusion.67
  365.9 4.0 %multiply_convert_fusion = bf16[2,1024,1024]{2,1,0:T(8,128)(2,1)} fusion(f32[2,1024,1024]{2,1,0:T(8,128)S(1)} %fusion.67, bf16[2,1024,192]{2,0,1:T(2,128)(2,1)S(1)} %get-tuple-element.48, bf16[2,512,192]{1,2,0:T(8,128)(2,1)S(1)} %bitcast.111, bf16[2,512,192]{1,2,0:T(8,128)(2,1)S(1)} %bitcast.104), kind=kOutput, calls=%fused_computation.40 | convolution fusion | flops 813170688 | bytes 14155776 | tf_op jit(solution)/shard_map/kpx,kqx->kpq/dot_general | solution.py:97
  (18 shorter events, 0.4 us)
Async XLA Ops:
  0.0 301.8 %copy-start = (s32[512]{0:T(512)S(1)}, s32[512]{0:T(512)}, u32[]{:S(2)}) copy-start(s32[512]{0:T(512)} %param.11) | copy-start | bytes 6148
  41.8 71.3 %copy-start.1 = (f32[8,512]{1,0:T(8,128)S(1)}, f32[8,512]{1,0:T(8,128)}, u32[]{:S(2)}) copy-start(f32[8,512]{1,0:T(8,128)} %param.9) | copy-start | bytes 49156
  153.7 142.1 %all-to-all-start.2 = ((bf16[2,8,2,32,192]{4,3,2,0,1:T(8,128)(2,1)}), bf16[2,8,2,32,192]{4,3,2,0,1:T(8,128)(2,1)S(1)}, u32[]{:S(2)}, u32[]{:S(2)}) async-start(bf16[2,8,2,32,192]{4,3,2,0,1:T(8,128)(2,1)} %copy.88), calls=%async_computation.2 | async-start | bytes 1048576 | tf_op jit(solution)/shard_map/all_to_all | solution.py:73
  295.7 20.0 %all-to-all-start = ((bf16[2,8,2,32,192]{4,3,2,0,1:T(8,128)(2,1)}), bf16[2,8,2,32,192]{4,3,2,0,1:T(8,128)(2,1)S(1)}, u32[]{:S(2)}, u32[]{:S(2)}) async-start(bf16[2,8,2,32,192]{4,3,2,0,1:T(8,128)(2,1)} %copy.77), calls=%async_computation | async-start | bytes 1048576 | tf_op jit(solution)/shard_map/all_to_all | solution.py:73
  315.7 9.3 %all-to-all-start.3 = ((bf16[2,1,2,256,192]{3,4,1,0,2:T(8,128)(2,1)}), bf16[2,1,2,256,192]{3,4,1,0,2:T(8,128)(2,1)S(1)}, u32[]{:S(2)}, u32[]{:S(2)}) async-start(bf16[2,1,2,256,192]{3,4,1,0,2:T(8,128)(2,1)} %copy.90), calls=%async_computation.3 | async-start | bytes 786432 | tf_op jit(solution)/shard_map/all_to_all | solution.py:72
  325.0 9.3 %all-to-all-start.1 = ((bf16[2,1,2,256,192]{3,4,1,0,2:T(8,128)(2,1)}), bf16[2,1,2,256,192]{3,4,1,0,2:T(8,128)(2,1)S(1)}, u32[]{:S(2)}, u32[]{:S(2)}) async-start(bf16[2,1,2,256,192]{3,4,1,0,2:T(8,128)(2,1)} %copy.79), calls=%async_computation.1 | async-start | bytes 786432 | tf_op jit(solution)/shard_map/all_to_all | solution.py:72
where the time goes:
time: 372 us; the launch traced here: 370 us
  local copies, waits for them, and re-layouts  231 us (62%)
  matrix products  76.5 us (21%)
  other arithmetic  23.7 us (6%)
  starting transfers between devices  20.2 us (5%)
  waiting for transfers between devices  12.7 us (3%)
  blocking collectives  4.96 us (1%)
    slice x2, local copies, waits for them, and re-layouts, shards(): signal[:, :, tap_index:tap_index + spec_len, :]  143 us
    dot_general x2, matrix products, shards(): jnp.einsum('iasj,ajbkg->kgibs', summed, table, precision=lax.Precision.HI...  70.9 us
    convert_element_type x2, local copies, waits for them, and re-layouts, shards(): volts[batch].astype(jnp.float32)  52.5 us
    convert_element_type x1, other arithmetic, shards(): volts[batch].astype(jnp.float32)  14.1 us
    all_to_all x2, starting transfers between devices, shards(): lax.all_to_all(result.reshape(CAP, chan_count, cols_count, local_inputs,...  13.3 us
    gather x2, local copies, waits for them, and re-layouts, shards(): columns = jnp.take(flat, located, axis=1)  12.7 us
  transfers between devices with their start and end apart: 4, of which 3 were waited for; matrix products, arithmetic and copies ran while one was open for 39% of the time, Pallas kernels for 0%

commit v1 on v0

--- a/solution.py
+++ b/solution.py
@@ -1,8 +1,12 @@
+import functools
 import math
 
 import jax
 import jax.numpy as jnp
+import numpy as np
 from jax import lax
+from jax.experimental import pallas as pl
+from jax.experimental.pallas import tpu as pltpu
 from jax.sharding import PartitionSpec as P
 
 STATIONS = 512
@@ -10,6 +14,7 @@
 TAPS = 8
 BATCHES = 2
 CAP = 2
+LANES = 128
 
 
 def slot_table(owner_map, owner_count, slot_count):
@@ -27,7 +32,7 @@
     return (channel, is_live)
 
 
-def shards(volts, taps, owner_map, assign):
+def general_shards(volts, taps, owner_map, assign):
     chan_count = lax.axis_size("chan")
     rows_count = lax.axis_size("row")
     cols_count = lax.axis_size("col")
@@ -101,8 +106,279 @@
     return (total * scale).reshape(CAP, 2, row_count, total_inputs).astype(jnp.bfloat16)
 
 
+def trig_table(channels):
+    points = np.arange(NFFT)
+    phase = (np.arange(channels)[:, None] * points[None, :] % NFFT) * (2.0 * math.pi / NFFT)
+    unit = 1.0 / math.sqrt(NFFT)
+    return np.concatenate([np.cos(phase), np.sin(phase)], axis=0).astype(np.float32) * np.float32(unit)
+
+
+BLOCK = 4
+AHEAD = 6
+LAG = 8
+
+
+def spectra_kernel(batch, channels, owners, inputs, rows, spec_len,
+                   owner_ref, volts_ref, taps_ref, trig_ref, out_ref,
+                   wave, weight, prod, lined, count, table, sem):
+    blocks = pl.cdiv(rows, BLOCK)
+    parts = NFFT // LANES
+    halves = 2 * channels
+    pairs = spec_len // 2
+    stride = lined.shape[0] // channels
+
+    def fetch(block):
+        for step in range(BLOCK):
+            row = jnp.minimum(block * BLOCK + step, rows - 1)
+            for part in range(parts):
+                start = pl.multiple_of(row * NFFT + part * LANES, LANES)
+                pltpu.make_async_copy(
+                    volts_ref.at[batch, :, :, pl.ds(start, LANES)],
+                    wave.at[block, part, pl.ds(step * inputs, inputs)],
+                    sem.at[block],
+                ).start()
+
+    def arrived(block):
+        pltpu.make_async_copy(wave.at[block], wave.at[block], sem.at[block]).wait()
+
+    for block in range(AHEAD):
+        fetch(block)
+
+    for tap in range(TAPS):
+        scaled = trig_ref[...] * taps_ref[tap:tap + 1, :]
+        high = scaled.astype(jnp.bfloat16)
+        low = (scaled - high.astype(jnp.float32)).astype(jnp.bfloat16)
+        weight[tap * halves:(tap + 1) * halves, :NFFT] = high
+        weight[tap * halves:(tap + 1) * halves, NFFT:] = low
+
+    for owner in range(owners):
+        count[owner] = 0
+        for slot in range(CAP):
+            table[owner * CAP + slot] = 0
+
+    @pl.loop(0, channels)
+    def _(k):
+        owner = owner_ref[k]
+        used = count[owner]
+        table[owner * CAP + used] = k
+        count[owner] = used + 1
+
+    lane = lax.broadcasted_iota(jnp.int32, (halves, LANES), 1)
+    low_half = lane < LANES // 2
+    even = (lax.broadcasted_iota(jnp.int32, (channels, LANES), 1) % 2) == 0
+
+    def tap_sum(tile, odd):
+        total = prod[tile, odd * halves:(odd + 1) * halves, :]
+        for e in range(1, TAPS // 2):
+            m = 2 * e + odd
+            total = total + prod[tile + e, m * halves:(m + 1) * halves, :]
+        return total
+
+    def finish(pair, turned):
+        for step in range(2):
+            tile = pair + step
+            following = pltpu.roll(tap_sum(tile + 1, 1), LANES // 2, 1)
+            value = tap_sum(tile, 0) + jnp.where(low_half, turned, following)
+            turned = following
+            cosine = value[:channels]
+            sine = value[channels:]
+            mixed = cosine + jnp.where(
+                even, pltpu.roll(sine, LANES - 1, 1), -pltpu.roll(sine, 1, 1)
+            )
+            lined[pl.ds(tile, channels, stride=stride), :] = mixed
+        return turned
+
+    def body(block, turned):
+        ahead = jnp.minimum(block + AHEAD, blocks - 1)
+
+        @pl.when(block + AHEAD < blocks)
+        def _():
+            fetch(ahead)
+
+        arrived(block)
+        turned = finish(2 * block + LAG - 6, turned)
+        x = jnp.concatenate(
+            [wave.at[block, part].reshape(BLOCK * inputs * 2, LANES)[...] for part in range(parts)],
+            axis=1,
+        )
+        y = lax.dot_general(
+            weight[...], jnp.concatenate([x, x], axis=1), (((1,), (1,)), ((), ())),
+            preferred_element_type=jnp.float32,
+        )
+        prod[2 * block + LAG] = y[:, :LANES]
+        prod[2 * block + LAG + 1] = y[:, LANES:]
+        return turned
+
+    turned = lax.fori_loop(0, blocks, body, jnp.zeros((halves, LANES), jnp.float32))
+    finish(2 * blocks + LAG - 6, turned)
+
+    span = LANES // 2
+    to = lax.broadcasted_iota(jnp.int32, (LANES, LANES), 0)
+    source = ((to // inputs) % 2) * span + (to % inputs) * 2 + to // (2 * inputs)
+    turn = (lax.broadcasted_iota(jnp.int32, (LANES, LANES), 1) == source).astype(jnp.bfloat16)
+    for owner in range(owners):
+        pieces = []
+        for slot in range(CAP):
+            k = table[owner * CAP + slot]
+            pieces.append(lined[pl.ds(k * stride + LAG, pairs), :].astype(jnp.bfloat16))
+        w = jnp.concatenate(pieces, axis=0)
+        t = lax.dot_general(turn, w, (((1,), (1,)), ((), ())), preferred_element_type=jnp.float32)
+        cols = []
+        for slot in range(CAP):
+            for q in range(4):
+                cols.append(t[q * inputs:(q + 1) * inputs, slot * pairs:(slot + 1) * pairs])
+        out_ref[owner] = jnp.concatenate(cols, axis=1).astype(jnp.bfloat16)
+
+
+def spectra(batch, volts, taps, owner_map, owners):
+    channels = owner_map.shape[0]
+    inputs = volts.shape[1]
+    rows = volts.shape[3] // NFFT
+    spec_len = rows - TAPS + 1
+    blocks = -(-rows // BLOCK)
+    halves = 2 * channels
+    parts = NFFT // LANES
+    stride = 2 * blocks + LAG
+    stride = -(-stride // 8) * 8
+    trig = jnp.asarray(trig_table(channels))
+    return pl.pallas_call(
+        functools.partial(spectra_kernel, batch, channels, owners, inputs, rows, spec_len),
+        out_shape=jax.ShapeDtypeStruct((owners, inputs, 2 * CAP * spec_len), jnp.bfloat16),
+        in_specs=[
+            pl.BlockSpec(memory_space=pltpu.SMEM),
+            pl.BlockSpec(memory_space=pl.ANY),
+            pl.BlockSpec(memory_space=pltpu.VMEM),
+            pl.BlockSpec(memory_space=pltpu.VMEM),
+        ],
+        out_specs=pl.BlockSpec(memory_space=pltpu.VMEM),
+        scratch_shapes=[
+            pltpu.VMEM((blocks, parts, BLOCK * inputs, 2, LANES), jnp.bfloat16),
+            pltpu.VMEM((TAPS * halves, 2 * NFFT), jnp.bfloat16),
+            pltpu.VMEM((2 * blocks + LAG, TAPS * halves, LANES), jnp.float32),
+            pltpu.VMEM((channels * stride, LANES), jnp.float32),
+            pltpu.SMEM((owners,), jnp.int32),
+            pltpu.SMEM((owners * CAP,), jnp.int32),
+            pltpu.SemaphoreType.DMA((blocks,)),
+        ],
+        compiler_params=pltpu.CompilerParams(vmem_limit_bytes=48 * 1024 * 1024),
+        cost_estimate=pl.CostEstimate(
+            flops=4 * rows * inputs * 2 * NFFT * TAPS * halves, bytes_accessed=volts.size, transcendentals=0
+        ),
+        name="spectra",
+    )(owner_map, volts, taps, trig)
+
+
+def visibility_kernel(scale, live_ref, place_ref, mine_a, mine_b, other_a, other_b, out_ref, cols, rows):
+    slot = pl.program_id(0)
+    step = pl.program_id(1)
+    half, width = mine_a.shape
+    total = 2 * half
+    group = width // CAP
+    high = -(-group // LANES) * LANES
+    row_count = out_ref.shape[2]
+
+    @pl.when((slot == 0) & (step == 0))
+    def _():
+        for index, (mine, other) in enumerate(((mine_a, other_a), (mine_b, other_b))):
+            got = jnp.dot(place_ref[:, :half], mine[...], preferred_element_type=jnp.float32)
+            got = got + jnp.dot(place_ref[:, half:], other[...], preferred_element_type=jnp.float32)
+            got = got.astype(jnp.bfloat16)
+            cols[index] = got
+
+    first = live_ref[1] + step * row_count
+    first = pl.multiple_of(first, row_count)
+    source = lax.broadcasted_iota(jnp.int32, (width, high), 0)
+    target = lax.broadcasted_iota(jnp.int32, (width, high), 1)
+    for s in range(CAP):
+        @pl.when(slot == s)
+        def _():
+            base = s * (width - high)
+            inside = target + base - s * group
+            ok = (inside >= 0) & (inside < group)
+            plain = jnp.where(ok & (source == target + base), 1.0, 0.0).astype(jnp.bfloat16)
+            part = group // 2
+            swapped = jnp.where(inside < part, target + base + part, target + base - part)
+            sign = jnp.where(inside < part, 1.0, -1.0)
+            turn = jnp.where(ok & (source == swapped), sign, 0.0).astype(jnp.bfloat16)
+            re = jnp.zeros((row_count, total), jnp.float32)
+            im = jnp.zeros((row_count, total), jnp.float32)
+            for index in range(BATCHES):
+                lead = cols[index, pl.ds(first, row_count), :]
+                a = jnp.dot(lead, plain, preferred_element_type=jnp.float32).astype(jnp.bfloat16)
+                f = jnp.dot(lead, turn, preferred_element_type=jnp.float32).astype(jnp.bfloat16)
+                c = cols[index, :, base:base + high]
+                dims = (((1,), (1,)), ((), ()))
+                re = re + lax.dot_general(a, c, dims, preferred_element_type=jnp.float32)
+                im = im + lax.dot_general(f, c, dims, preferred_element_type=jnp.float32)
+            live = s < live_ref[0]
+            out_ref[0, 0] = jnp.where(live, re * scale, 0.0).astype(jnp.bfloat16)
+            out_ref[0, 1] = jnp.where(live, im * scale, 0.0).astype(jnp.bfloat16)
+
+
+def visibility(scale, live, place, mine, other, row_count):
+    half, width = mine[0].shape
+    total = 2 * half
+    block = 128
+    return pl.pallas_call(
+        functools.partial(visibility_kernel, scale),
+        out_shape=jax.ShapeDtypeStruct((CAP, 2, row_count, total), jnp.bfloat16),
+        grid=(CAP, row_count // block),
+        in_specs=[pl.BlockSpec(memory_space=pltpu.SMEM)]
+        + [pl.BlockSpec(memory_space=pltpu.VMEM)] * 5,
+        out_specs=pl.BlockSpec((1, 2, block, total), lambda s, p: (s, 0, p, 0)),
+        scratch_shapes=[
+            pltpu.VMEM((BATCHES, total, width), jnp.bfloat16),
+            pltpu.VMEM((8, LANES), jnp.float32),
+        ],
+        compiler_params=pltpu.CompilerParams(vmem_limit_bytes=48 * 1024 * 1024),
+        name="visibility",
+    )(live, place, *mine, *other)
+
+
+def tiled_shards(volts, taps, owner_map, assign):
+    chan_count = lax.axis_size("chan")
+    rows_count = lax.axis_size("row")
+    cols_count = lax.axis_size("col")
+    owners = chan_count * cols_count
+    inputs = volts.shape[1]
+    spec_len = volts.shape[3] // NFFT - TAPS + 1
+    my_row = lax.axis_index("row")
+    me = lax.axis_index("chan") * cols_count + lax.axis_index("col")
+    total_inputs = 2 * STATIONS
+    row_count = total_inputs // rows_count
+    positions = jnp.arange(total_inputs, dtype=jnp.int32)
+    pick = 2 * jnp.repeat(assign, 2) + positions % 2
+    device_of = pick // inputs
+    within = pick % inputs
+    chan_of = device_of // (rows_count * cols_count)
+    row_of = device_of // cols_count % rows_count
+    col_of = device_of % cols_count
+    located = (
+        jnp.where(row_of == my_row, 0, owners) + chan_of * cols_count + col_of
+    ) * inputs + within
+    place = (located[:, None] == positions[None, :]).astype(jnp.bfloat16)
+    owned = jnp.sum((owner_map == me).astype(jnp.int32))
+    live = jnp.stack([owned, my_row * row_count])
+    mine = []
+    other = []
+    for batch in range(BATCHES):
+        sent = spectra(batch, volts, taps, owner_map, owners)
+        turned = lax.all_to_all(sent, ("chan", "col"), split_axis=0, concat_axis=0, tiled=True)
+        flat = turned.reshape(owners * inputs, -1)
+        mine.append(flat)
+        other.append(lax.ppermute(flat, "row", [(0, 1), (1, 0)]))
+    scale = 1.0 / math.sqrt(2 * BATCHES * spec_len)
+    return visibility(scale, live, place, mine, other, row_count)
+
+
 def solution(mesh):
     placed = (P(None, ("chan", "row", "col"), None, None), P(), P(), P())
+
+    def shards(volts, taps, owner_map, assign):
+        if 4 * volts.shape[1] == LANES and mesh.shape["row"] == 2:
+            return tiled_shards(volts, taps, owner_map, assign)
+        return general_shards(volts, taps, owner_map, assign)
+
     return jax.shard_map(
         shards,
         mesh=mesh,

time: 372 us -> 74.1 us (0.20)
  local copies, waits for them, and re-layouts: 231 us -> 2.57 us
  matrix products: 76.5 us -> 0 us
  Pallas kernels: 0 us -> 42.1 us
  other arithmetic: 23.7 us -> 1.81 us
  blocking collectives: 4.96 us -> 0 us
  starting transfers between devices: 20.2 us -> 15.3 us
    slice x3 -> x0, local copies, waits for them, and re-layouts: 143 us -> none  [the longest x2 143 us: shards(): signal[:, :, tap_index:tap_index + spec_len, :]]
    dot_general x4 -> x0, matrix products: 76.5 us -> none  [the longest x2 70.9 us: shards(): jnp.einsum('iasj,ajbkg->kgibs', summed, table, precision=lax.Precision.HI...]
    convert_element_type x8 -> x0, local copies, waits for them, and re-layouts: 55.9 us -> none  [the longest x2 52.5 us: shards(): volts[batch].astype(jnp.float32)]
    pallas_call x0 -> x3, Pallas kernels: none -> 42.1 us  [the longest x2 30.1 us: spectra(): pl.pallas_call(functools.partial(spectra_kernel, batch, channels, owners,...]
    gather x9 -> x0, local copies, waits for them, and re-layouts: 27.6 us -> none  [the longest x2 12.7 us: shards(): columns = jnp.take(flat, located, axis=1)]
    convert_element_type x1, other arithmetic: 14.1 us -> 0.4 us  [tiled_shards(): place = (located[:, None] == positions[None, :]).astype(jnp.bfloat16)]
    select_n x5 -> x0, other arithmetic: 5.79 us -> none  [the longest x1 5.54 us: shards(): columns = jnp.take(flat, located, axis=1)]
    all_to_all x4 -> x2, starting transfers between devices: 20.2 us -> 15.3 us  [tiled_shards(): lax.all_to_all(sent, ('chan', 'col'), split_axis=0, concat_axis=0, tiled=...]
  transfers between devices with their start and end apart: 4 -> 4, of which waited for: 3 -> 1; matrix products, arithmetic and copies ran while one was open for 39% -> 3% of each run, Pallas kernels for 0% -> 21%
where the time goes in v1:
time: 74.1 us; the launch traced here: 73.5 us
  Pallas kernels  42.1 us (57%)
  starting transfers between devices  15.3 us (21%)
  waiting for transfers between devices  11.6 us (16%)
  local copies, waits for them, and re-layouts  2.57 us (3%)
  other arithmetic  1.81 us (2%)
    pallas_call x2, Pallas kernels, spectra(): pl.pallas_call(functools.partial(spectra_kernel, batch, channels, owners,...  30.1 us
    all_to_all x2, starting transfers between devices, tiled_shards(): lax.all_to_all(sent, ('chan', 'col'), split_axis=0, concat_axis=0, tiled=...  15.3 us
    pallas_call x1, Pallas kernels, visibility(): pl.pallas_call(functools.partial(visibility_kernel, scale), out_shape=jax...  11.9 us
    all_to_all x2, waiting for transfers between devices, tiled_shards(): lax.all_to_all(sent, ('chan', 'col'), split_axis=0, concat_axis=0, tiled=...  11.6 us
    unnamed x14, local copies, waits for them, and re-layouts  2.28 us
  transfers between devices with their start and end apart: 4, of which 1 were waited for; matrix products, arithmetic and copies ran while one was open for 3% of the time, Pallas kernels for 21%

profile of v1, /device:TPU:0, one launch (start us, length us, event | category | flops | bytes accessed | tf_op | source)
XLA Modules:
  0.0 73.5 jit_solution(629784797795218601)
XLA Ops:
  0.0 0.0 copy-start
  0.0 0.7 copy-done
  0.7 0.0 copy-start.2
  0.7 0.7 copy-done.2
  1.4 0.0 copy-start.4
  1.4 0.9 %copy-done.4 = f32[48,512]{1,0:T(8,128)S(1)} copy-done((f32[48,512]{1,0:T(8,128)S(1)}, f32[48,512]{1,0:T(8,128)}, u32[]{:S(2)}) %copy-start.4) | copy-done | bytes 98328
  2.3 0.0 copy-start.1
  2.3 0.0 copy-start.3
  2.3 0.0 copy-start.5
  2.3 15.0 %spectra.2 = bf16[16,32,384]{2,1,0:T(8,128)(2,1)} custom-call(s32[24]{0:T(128)S(1)} %copy-done.2, bf16[2,32,2,52736]{3,2,1,0:T(2,128)(2,1)} %volts_ref.3, f32[8,512]{1,0:T(8,128)S(1)} %copy-done, f32[48,512]{1,0:T(8,128)S(1)} %copy-done.4), custom_call_target="tpu_custom_call" | custom-call | flops 5184159744 | bytes 6750208 | tf_op jit(solution)/shard_map/spectra/pallas_call | solution.py:244
  17.3 8.3 %all-to-all-start = ((bf16[16,32,384]{2,1,0:T(8,128)(2,1)}), bf16[16,32,384]{2,1,0:T(8,128)(2,1)S(1)}, u32[]{:S(2)}, u32[]{:S(2)}) async-start(bf16[16,32,384]{2,1,0:T(8,128)(2,1)} %spectra.2), calls=%async_computation | async-start | bytes 786432 | tf_op jit(solution)/shard_map/all_to_all | solution.py:366
  25.6 0.0 copy-done.1
  25.6 0.0 copy-done.3
  25.6 0.0 copy-done.5
  25.6 0.0 copy-start.6
  25.7 15.1 %spectra.3 = bf16[16,32,384]{2,1,0:T(8,128)(2,1)} custom-call(s32[24]{0:T(128)S(1)} %copy-done.3, bf16[2,32,2,52736]{3,2,1,0:T(2,128)(2,1)} %volts_ref.3, f32[8,512]{1,0:T(8,128)S(1)} %copy-done.1, f32[48,512]{1,0:T(8,128)S(1)} %copy-done.5), custom_call_target="tpu_custom_call" | custom-call | flops 5184159744 | bytes 6750208 | tf_op jit(solution)/shard_map/spectra/pallas_call | solution.py:244
  40.8 0.0 all-to-all-done
  40.8 6.9 %all-to-all-start.1 = ((bf16[16,32,384]{2,1,0:T(8,128)(2,1)}), bf16[16,32,384]{2,1,0:T(8,128)(2,1)S(1)}, u32[]{:S(2)}, u32[]{:S(2)}) async-start(bf16[16,32,384]{2,1,0:T(8,128)(2,1)} %spectra.3), calls=%async_computation.1 | async-start | bytes 786432 | tf_op jit(solution)/shard_map/all_to_all | solution.py:366
  47.7 0.0 copy-done.6
  47.8 0.1 broadcast_in_dim.11
  47.9 0.2 mul.35
  48.1 0.1 collective-permute-start
  48.2 11.6 %all-to-all-done.1 = bf16[16,32,384]{2,1,0:T(8,128)(2,1)S(1)} async-done(((bf16[16,32,384]{2,1,0:T(8,128)(2,1)}), bf16[16,32,384]{2,1,0:T(8,128)(2,1)S(1)}, u32[]{:S(2)}, u32[]{:S(2)}) %all-to-all-start.1) | async-done | bytes 393248 | tf_op jit(solution)/shard_map/all_to_all | solution.py:366
  59.8 0.0 collective-permute-start.1
  59.8 0.7 fusion.18
  60.4 0.7 pad_add_fusion.live_ref
  61.1 0.4 fusion.place_ref
  61.5 0.0 collective-permute-done.other_a
  61.6 0.0 collective-permute-done.1.other_b
  61.6 11.9 %visibility.1 = bf16[2,2,512,1024]{3,2,1,0:T(8,128)(2,1)} custom-call(s32[2]{0:T(128)S(1)} %pad_add_fusion.live_ref, bf16[1024,1024]{1,0:T(8,128)(2,1)S(1)} %fusion.place_ref, bf16[512,384]{1,0:T(8,128)(2,1)S(1)} %bitcast.5, bf16[512,384]{1,0:T(8,128)(2,1)S(1)} %bitcast.7, bf16[512,384]{1,0:T(8,128)(2,1)S(1)} %collective-permute-done.other_a, ...), custom_call_target="tpu_custom_call" | custom-call | tf_op jit(solution)/shard_map/visibility/pallas_call | solution.py:322
  (2 shorter events, 0.0 us)
Async XLA Ops:
  0.0 0.7 copy-start
  0.7 0.7 copy-start.2
  1.4 0.9 %copy-start.4 = (f32[48,512]{1,0:T(8,128)S(1)}, f32[48,512]{1,0:T(8,128)}, u32[]{:S(2)}) copy-start(f32[48,512]{1,0:T(8,128)} %constant.88.clone.trig_ref) | copy-start | bytes 294916
  2.3 23.3 %copy-start.1 = (f32[8,512]{1,0:T(8,128)S(1)}, f32[8,512]{1,0:T(8,128)}, u32[]{:S(2)}) copy-start(f32[8,512]{1,0:T(8,128)} %taps_ref.3) | copy-start | bytes 49156
  2.3 23.4 %copy-start.3 = (s32[24]{0:T(128)S(1)}, s32[24]{0:T(128)}, u32[]{:S(2)}) copy-start(s32[24]{0:T(128)} %owner_ref.3) | copy-start | bytes 292
  2.3 23.4 %copy-start.5 = (f32[48,512]{1,0:T(8,128)S(1)}, f32[48,512]{1,0:T(8,128)}, u32[]{:S(2)}) copy-start(f32[48,512]{1,0:T(8,128)} %constant.88.clone.trig_ref) | copy-start | bytes 294916
  17.3 23.5 %all-to-all-start = ((bf16[16,32,384]{2,1,0:T(8,128)(2,1)}), bf16[16,32,384]{2,1,0:T(8,128)(2,1)S(1)}, u32[]{:S(2)}, u32[]{:S(2)}) async-start(bf16[16,32,384]{2,1,0:T(8,128)(2,1)} %spectra.2), calls=%async_computation | async-start | bytes 786432 | tf_op jit(solution)/shard_map/all_to_all | solution.py:366
  25.6 22.1 %copy-start.6 = (s32[512]{0:T(512)S(1)}, s32[512]{0:T(512)}, u32[]{:S(2)}) copy-start(s32[512]{0:T(512)} %param.9) | copy-start | bytes 6148
  40.8 19.0 %all-to-all-start.1 = ((bf16[16,32,384]{2,1,0:T(8,128)(2,1)}), bf16[16,32,384]{2,1,0:T(8,128)(2,1)S(1)}, u32[]{:S(2)}, u32[]{:S(2)}) async-start(bf16[16,32,384]{2,1,0:T(8,128)(2,1)} %spectra.3), calls=%async_computation.1 | async-start | bytes 786432 | tf_op jit(solution)/shard_map/all_to_all | solution.py:366
  48.1 13.5 %collective-permute-start = (bf16[512,384]{1,0:T(8,128)(2,1)S(1)}, bf16[512,384]{1,0:T(8,128)(2,1)S(1)}, u32[]{:S(2)}, u32[]{:S(2)}) collective-permute-start(bf16[512,384]{1,0:T(8,128)(2,1)S(1)} %bitcast.4), channel_id=1, source_target_pairs={{0,2},{2,0},{1,3},{3,1},{4,6},{6,4},{5,7},{7,5},{8,10},{10,8},{9,1... | collective-permute-start | bytes 1179656 | tf_op jit(solution)/shard_map/ppermute | solution.py:369
  59.8 1.8 %collective-permute-start.1 = (bf16[512,384]{1,0:T(8,128)(2,1)S(1)}, bf16[512,384]{1,0:T(8,128)(2,1)S(1)}, u32[]{:S(2)}, u32[]{:S(2)}) collective-permute-start(bf16[512,384]{1,0:T(8,128)(2,1)S(1)} %bitcast.6), channel_id=1, source_target_pairs={{0,2},{2,0},{1,3},{3,1},{4,6},{6,4},{5,7},{7,5},{8,10},{10,8},{9,1... | collective-permute-start | bytes 1179656 | tf_op jit(solution)/shard_map/ppermute | solution.py:369

commit v2 on v1

--- a/solution.py
+++ b/solution.py
@@ -114,35 +114,50 @@
 
 
 BLOCK = 4
-AHEAD = 6
+MXU = 256
+UNROLL = 2
+UNIT = 16
+ORDER = ((0, 1, 2, 0, 1, 2, 0, 1), (0, 1, 0, 2, 2, 1, 0, 1))
+LAYOUT = (
+    ((0, 0, (0, 1, 2)), (0, 1, (3, 4, 5)), (0, 2, (6, 7))),
+    ((1, 3, (4, 6, 7)), (0, 3, (0, 1, 2)), (0, 2, (5,)), (1, 2, (3,))),
+    ((1, 0, (0, 1, 3)), (1, 1, (2, 4, 5)), (1, 2, (6, 7))),
+)
 LAG = 8
 
 
 def spectra_kernel(batch, channels, owners, inputs, rows, spec_len,
-                   owner_ref, volts_ref, taps_ref, trig_ref, out_ref,
-                   wave, weight, prod, lined, count, table, sem):
-    blocks = pl.cdiv(rows, BLOCK)
-    parts = NFFT // LANES
+                   owner_hbm, volts_ref, taps_hbm, trig_hbm, out_ref,
+                   wave, weight, prod, lined, taps_ref, trig_ref,
+                   owner_ref, count, table, sem, small):
+    blocks = wave.shape[0]
     halves = 2 * channels
     pairs = spec_len // 2
     stride = lined.shape[0] // channels
-
-    def fetch(block):
+    lanes = 2 * inputs
+    source = volts_ref.at[batch].reshape(lanes, volts_ref.shape[3])
+
+    loads = [
+        pltpu.make_async_copy(taps_hbm, taps_ref, small.at[0]),
+        pltpu.make_async_copy(trig_hbm, trig_ref, small.at[1]),
+        pltpu.make_async_copy(owner_hbm, owner_ref, small.at[2]),
+    ]
+    for load in loads:
+        load.start()
+
+    @pl.loop(0, blocks)
+    def _(block):
         for step in range(BLOCK):
             row = jnp.minimum(block * BLOCK + step, rows - 1)
-            for part in range(parts):
-                start = pl.multiple_of(row * NFFT + part * LANES, LANES)
-                pltpu.make_async_copy(
-                    volts_ref.at[batch, :, :, pl.ds(start, LANES)],
-                    wave.at[block, part, pl.ds(step * inputs, inputs)],
-                    sem.at[block],
-                ).start()
-
-    def arrived(block):
-        pltpu.make_async_copy(wave.at[block], wave.at[block], sem.at[block]).wait()
-
-    for block in range(AHEAD):
-        fetch(block)
+            start = pl.multiple_of(row * NFFT, NFFT)
+            pltpu.make_async_copy(
+                source.at[:, pl.ds(start, NFFT)],
+                wave.at[block, pl.ds(step * lanes, lanes)],
+                sem.at[block],
+            ).start()
+
+    for load in loads:
+        load.wait()
 
     for tap in range(TAPS):
         scaled = trig_ref[...] * taps_ref[tap:tap + 1, :]
@@ -155,13 +170,7 @@
         count[owner] = 0
         for slot in range(CAP):
             table[owner * CAP + slot] = 0
-
-    @pl.loop(0, channels)
-    def _(k):
-        owner = owner_ref[k]
-        used = count[owner]
-        table[owner * CAP + used] = k
-        count[owner] = used + 1
+    table[owners * CAP] = 0
 
     lane = lax.broadcasted_iota(jnp.int32, (halves, LANES), 1)
     low_half = lane < LANES // 2
@@ -175,7 +184,7 @@
         return total
 
     def finish(pair, turned):
-        for step in range(2):
+        for step in range(2 * UNROLL):
             tile = pair + step
             following = pltpu.roll(tap_sum(tile + 1, 1), LANES // 2, 1)
             value = tap_sum(tile, 0) + jnp.where(low_half, turned, following)
@@ -188,46 +197,128 @@
             lined[pl.ds(tile, channels, stride=stride), :] = mixed
         return turned
 
-    def body(block, turned):
-        ahead = jnp.minimum(block + AHEAD, blocks - 1)
-
-        @pl.when(block + AHEAD < blocks)
-        def _():
-            fetch(ahead)
-
-        arrived(block)
-        turned = finish(2 * block + LAG - 6, turned)
-        x = jnp.concatenate(
-            [wave.at[block, part].reshape(BLOCK * inputs * 2, LANES)[...] for part in range(parts)],
-            axis=1,
-        )
-        y = lax.dot_general(
-            weight[...], jnp.concatenate([x, x], axis=1), (((1,), (1,)), ((), ())),
-            preferred_element_type=jnp.float32,
-        )
-        prod[2 * block + LAG] = y[:, :LANES]
-        prod[2 * block + LAG + 1] = y[:, LANES:]
-        return turned
-
-    turned = lax.fori_loop(0, blocks, body, jnp.zeros((halves, LANES), jnp.float32))
-    finish(2 * blocks + LAG - 6, turned)
-
-    span = LANES // 2
-    to = lax.broadcasted_iota(jnp.int32, (LANES, LANES), 0)
-    source = ((to // inputs) % 2) * span + (to % inputs) * 2 + to // (2 * inputs)
-    turn = (lax.broadcasted_iota(jnp.int32, (LANES, LANES), 1) == source).astype(jnp.bfloat16)
-    for owner in range(owners):
-        pieces = []
-        for slot in range(CAP):
-            k = table[owner * CAP + slot]
-            pieces.append(lined[pl.ds(k * stride + LAG, pairs), :].astype(jnp.bfloat16))
-        w = jnp.concatenate(pieces, axis=0)
-        t = lax.dot_general(turn, w, (((1,), (1,)), ((), ())), preferred_element_type=jnp.float32)
-        cols = []
-        for slot in range(CAP):
-            for q in range(4):
-                cols.append(t[q * inputs:(q + 1) * inputs, slot * pairs:(slot + 1) * pairs])
-        out_ref[owner] = jnp.concatenate(cols, axis=1).astype(jnp.bfloat16)
+    def place(k):
+        real = k < channels
+        owner = owner_ref[jnp.minimum(k, channels - 1)]
+        used = count[owner]
+        table[jnp.where(real, owner * CAP + used, owners * CAP)] = k
+        count[owner] = jnp.where(real, used + 1, used)
+
+    def wait(first):
+        for step in range(UNROLL):
+            pltpu.make_async_copy(wave.at[first + step], wave.at[first + step], sem.at[first + step]).wait()
+
+    def stage(first, part):
+        for step in range(UNROLL):
+            x = wave[first + step, :, part * MXU:(part + 1) * MXU]
+            pltpu.matmul_push_rhs(x, part, step, transpose=True)
+
+    def multiply(totals, following):
+        for part in range(NFFT // MXU):
+            for total in totals:
+                pltpu.matmul_acc_lhs(
+                    total, weight[:, part * MXU:(part + 1) * MXU], load_staged_rhs=part
+                )
+            if following is not None:
+                stage(following, part)
+            for total in totals:
+                pltpu.matmul_acc_lhs(
+                    total, weight[:, NFFT + part * MXU:NFFT + (part + 1) * MXU]
+                )
+
+    def collect(first, totals):
+        for step, total in enumerate(totals):
+            y = pltpu.matmul_pop(total)
+            prod[2 * (first + step) + LAG] = y[:, :LANES]
+            prod[2 * (first + step) + LAG + 1] = y[:, LANES:]
+
+    def run(*totals):
+        even_totals = totals[:2]
+        odd_totals = totals[2:]
+
+        rounds = blocks // (2 * UNROLL) - 1
+        share = pl.cdiv(channels, rounds)
+
+        def body(group, turned):
+            first = group * 2 * UNROLL
+            wait(first + 2 * UNROLL)
+            wait(first + 3 * UNROLL)
+            for extra in range(share):
+                place(group * share + extra)
+            multiply(odd_totals, first + 2 * UNROLL)
+            turned = finish(2 * first + LAG - 4 - 2 * UNROLL, turned)
+            collect(first, even_totals)
+            multiply(even_totals, first + 3 * UNROLL)
+            turned = finish(2 * first + LAG - 4, turned)
+            collect(first + UNROLL, odd_totals)
+            return turned
+
+        wait(0)
+        wait(UNROLL)
+        for part in range(NFFT // MXU):
+            stage(0, part)
+        multiply(even_totals, UNROLL)
+        turned = lax.fori_loop(0, rounds, body, jnp.zeros((halves, LANES), jnp.float32))
+        first = rounds * 2 * UNROLL
+        wait(first + 2 * UNROLL)
+        multiply(odd_totals, first + 2 * UNROLL)
+        turned = finish(2 * first + LAG - 4 - 2 * UNROLL, turned)
+        collect(first, even_totals)
+        multiply(even_totals, None)
+        turned = finish(2 * first + LAG - 4, turned)
+        collect(first + UNROLL, odd_totals)
+        turned = finish(2 * first + LAG - 4 + 2 * UNROLL, turned)
+        collect(first + 2 * UNROLL, even_totals)
+        finish(2 * first + LAG - 4 + 4 * UNROLL, turned)
+
+    shape = (TAPS * halves, MXU)
+    pl.run_scoped(run, *(pltpu.ACC(mxu_id=index % 2)(shape, jnp.float32) for index in range(4)))
+
+    to = lax.broadcasted_iota(jnp.int32, (2 * LANES, MXU), 0)
+    at = lax.broadcasted_iota(jnp.int32, (2 * LANES, MXU), 1)
+    row = to % LANES
+    origin = ((row // inputs) % 2) * lanes + (row % inputs) * 2 + row // lanes + to - row
+    turn = (at == origin).astype(jnp.bfloat16)
+    unit = lax.broadcasted_iota(jnp.int32, (inputs, LANES), 1) // UNIT
+
+    def pick(choices, tile):
+        value = None
+        for column, group, units in choices:
+            piece = tile[group * inputs:(group + 1) * inputs, column * LANES:(column + 1) * LANES]
+            if value is None:
+                value = piece
+            else:
+                inside = functools.reduce(jnp.logical_or, [unit == u for u in units])
+                value = jnp.where(inside, piece, value)
+        return value
+
+    def deal(*totals):
+        for pair in range(owners // 2):
+            total = totals[pair % len(totals)]
+            sides = []
+            for side in range(2):
+                owner = 2 * pair + side
+                pieces = []
+                for slot in range(CAP):
+                    first = table[owner * CAP + slot] * stride + LAG
+                    for u in ORDER[slot]:
+                        start = pl.multiple_of(first + u * UNIT, 8)
+                        pieces.append(lined[pl.ds(start, UNIT), :].astype(jnp.bfloat16))
+                sides.append(jnp.concatenate(pieces, axis=0))
+            pltpu.matmul_push_rhs(
+                jnp.concatenate(sides, axis=1), pair // 2 % 2, pair % 2, transpose=True
+            )
+            pltpu.matmul_acc_lhs(total, turn, load_staged_rhs=pair // 2 % 2)
+            dealt = pltpu.matmul_pop(total)
+            for side in range(2):
+                tile = dealt[side * LANES:(side + 1) * LANES]
+                out_ref[2 * pair + side] = jnp.concatenate(
+                    [pick(choices, tile).astype(jnp.bfloat16) for choices in LAYOUT], axis=1
+                )
+
+    pl.run_scoped(
+        deal, *(pltpu.ACC(mxu_id=index % 2)((2 * LANES, MXU), jnp.float32) for index in range(4))
+    )
 
 
 def spectra(batch, volts, taps, owner_map, owners):
@@ -237,102 +328,118 @@
     spec_len = rows - TAPS + 1
     blocks = -(-rows // BLOCK)
     halves = 2 * channels
-    parts = NFFT // LANES
     stride = 2 * blocks + LAG
     stride = -(-stride // 8) * 8
     trig = jnp.asarray(trig_table(channels))
+    hbm = pl.BlockSpec(memory_space=pltpu.HBM)
     return pl.pallas_call(
         functools.partial(spectra_kernel, batch, channels, owners, inputs, rows, spec_len),
         out_shape=jax.ShapeDtypeStruct((owners, inputs, 2 * CAP * spec_len), jnp.bfloat16),
-        in_specs=[
-            pl.BlockSpec(memory_space=pltpu.SMEM),
-            pl.BlockSpec(memory_space=pl.ANY),
-            pl.BlockSpec(memory_space=pltpu.VMEM),
-            pl.BlockSpec(memory_space=pltpu.VMEM),
-        ],
+        in_specs=[hbm] * 4,
         out_specs=pl.BlockSpec(memory_space=pltpu.VMEM),
         scratch_shapes=[
-            pltpu.VMEM((blocks, parts, BLOCK * inputs, 2, LANES), jnp.bfloat16),
+            pltpu.VMEM((blocks, BLOCK * inputs * 2, NFFT), jnp.bfloat16),
             pltpu.VMEM((TAPS * halves, 2 * NFFT), jnp.bfloat16),
             pltpu.VMEM((2 * blocks + LAG, TAPS * halves, LANES), jnp.float32),
             pltpu.VMEM((channels * stride, LANES), jnp.float32),
+            pltpu.VMEM(taps.shape, jnp.float32),
+            pltpu.VMEM(trig.shape, jnp.float32),
+            pltpu.SMEM((channels,), jnp.int32),
             pltpu.SMEM((owners,), jnp.int32),
-            pltpu.SMEM((owners * CAP,), jnp.int32),
+            pltpu.SMEM((owners * CAP + 1,), jnp.int32),
             pltpu.SemaphoreType.DMA((blocks,)),
+            pltpu.SemaphoreType.DMA((3,)),
         ],
         compiler_params=pltpu.CompilerParams(vmem_limit_bytes=48 * 1024 * 1024),
         cost_estimate=pl.CostEstimate(
             flops=4 * rows * inputs * 2 * NFFT * TAPS * halves, bytes_accessed=volts.size, transcendentals=0
         ),
         name="spectra",
-    )(owner_map, volts, taps, trig)
-
-
-def visibility_kernel(scale, live_ref, place_ref, mine_a, mine_b, other_a, other_b, out_ref, cols, rows):
+    )(*(pltpu.with_memory_space_constraint(x, pltpu.HBM) for x in (owner_map, volts, taps, trig)))
+
+
+def lane_tables():
+    window = 2 * LANES
+    held = {}
+    for tile, choices in enumerate(LAYOUT):
+        for slot, quarter, units in choices:
+            for u in units:
+                for offset in range(UNIT):
+                    lane = tile * LANES + u * UNIT + offset
+                    held[slot, quarter, ORDER[slot][u], offset] = lane
+    keep = np.zeros((CAP, UNIT, window), np.float32)
+    turn = np.zeros((CAP, window, window), np.float32)
+    for (slot, quarter, third, offset), lane in held.items():
+        base = slot * LANES
+        other = held[slot, (quarter + 2) % 4, third, offset]
+        keep[slot, :, lane - base] = 1.0
+        turn[slot, other - base, lane - base] = 1.0 if quarter < 2 else -1.0
+    return keep, turn
+
+
+def visibility_kernel(scale, owner_ref, place_ref, keep_ref, turn_ref,
+                      mine_a, mine_b, other_a, other_b, out_ref, cols, lead):
     slot = pl.program_id(0)
     step = pl.program_id(1)
-    half, width = mine_a.shape
-    total = 2 * half
-    group = width // CAP
-    high = -(-group // LANES) * LANES
+    half = mine_a.shape[0]
     row_count = out_ref.shape[2]
+    block = out_ref.shape[3]
+    window = turn_ref.shape[1]
+    dims = (((1,), (1,)), ((), ()))
 
     @pl.when((slot == 0) & (step == 0))
     def _():
         for index, (mine, other) in enumerate(((mine_a, other_a), (mine_b, other_b))):
             got = jnp.dot(place_ref[:, :half], mine[...], preferred_element_type=jnp.float32)
             got = got + jnp.dot(place_ref[:, half:], other[...], preferred_element_type=jnp.float32)
-            got = got.astype(jnp.bfloat16)
-            cols[index] = got
-
-    first = live_ref[1] + step * row_count
-    first = pl.multiple_of(first, row_count)
-    source = lax.broadcasted_iota(jnp.int32, (width, high), 0)
-    target = lax.broadcasted_iota(jnp.int32, (width, high), 1)
+            cols[index] = got.astype(jnp.bfloat16)
+        first = pl.multiple_of(lax.axis_index("row") * row_count, row_count)
+        for s in range(CAP):
+            for index in range(BATCHES):
+                rows = cols[index, pl.ds(first, row_count), s * LANES:s * LANES + window]
+                lead[s, index, :row_count] = rows * keep_ref[s, :1]
+                lead[s, index, row_count:] = jnp.dot(
+                    rows, turn_ref[s], preferred_element_type=jnp.float32
+                ).astype(jnp.bfloat16)
+
+    me = lax.axis_index("chan") * lax.axis_size("col") + lax.axis_index("col")
+    owned = jnp.int32(0)
+    for k in range(owner_ref.shape[0]):
+        owned = owned + jnp.where(owner_ref[k] == me, 1, 0)
+    factor = jnp.where(slot < owned, jnp.float32(scale), jnp.float32(0.0))
+    at = pl.multiple_of(step * block, block)
     for s in range(CAP):
         @pl.when(slot == s)
         def _():
-            base = s * (width - high)
-            inside = target + base - s * group
-            ok = (inside >= 0) & (inside < group)
-            plain = jnp.where(ok & (source == target + base), 1.0, 0.0).astype(jnp.bfloat16)
-            part = group // 2
-            swapped = jnp.where(inside < part, target + base + part, target + base - part)
-            sign = jnp.where(inside < part, 1.0, -1.0)
-            turn = jnp.where(ok & (source == swapped), sign, 0.0).astype(jnp.bfloat16)
-            re = jnp.zeros((row_count, total), jnp.float32)
-            im = jnp.zeros((row_count, total), jnp.float32)
+            value = None
             for index in range(BATCHES):
-                lead = cols[index, pl.ds(first, row_count), :]
-                a = jnp.dot(lead, plain, preferred_element_type=jnp.float32).astype(jnp.bfloat16)
-                f = jnp.dot(lead, turn, preferred_element_type=jnp.float32).astype(jnp.bfloat16)
-                c = cols[index, :, base:base + high]
-                dims = (((1,), (1,)), ((), ()))
-                re = re + lax.dot_general(a, c, dims, preferred_element_type=jnp.float32)
-                im = im + lax.dot_general(f, c, dims, preferred_element_type=jnp.float32)
-            live = s < live_ref[0]
-            out_ref[0, 0] = jnp.where(live, re * scale, 0.0).astype(jnp.bfloat16)
-            out_ref[0, 1] = jnp.where(live, im * scale, 0.0).astype(jnp.bfloat16)
-
-
-def visibility(scale, live, place, mine, other, row_count):
+                c = cols[index, pl.ds(at, block), s * LANES:s * LANES + window]
+                term = lax.dot_general(lead[s, index], c, dims, preferred_element_type=jnp.float32)
+                value = term if value is None else value + term
+            value = (value * factor).astype(jnp.bfloat16)
+            out_ref[0, 0] = value[:row_count]
+            out_ref[0, 1] = value[row_count:]
+
+
+def visibility(scale, owner_map, place, mine, other, row_count):
     half, width = mine[0].shape
     total = 2 * half
-    block = 128
+    block = 256
+    keep, turn = (jnp.asarray(t, jnp.bfloat16) for t in lane_tables())
     return pl.pallas_call(
         functools.partial(visibility_kernel, scale),
         out_shape=jax.ShapeDtypeStruct((CAP, 2, row_count, total), jnp.bfloat16),
-        grid=(CAP, row_count // block),
+        grid=(CAP, total // block),
         in_specs=[pl.BlockSpec(memory_space=pltpu.SMEM)]
-        + [pl.BlockSpec(memory_space=pltpu.VMEM)] * 5,
-        out_specs=pl.BlockSpec((1, 2, block, total), lambda s, p: (s, 0, p, 0)),
+        + [pl.BlockSpec(memory_space=pltpu.VMEM)] * 7,
+        out_specs=pl.BlockSpec((1, 2, row_count, block), lambda s, p: (s, 0, 0, p)),
         scratch_shapes=[
             pltpu.VMEM((BATCHES, total, width), jnp.bfloat16),
-            pltpu.VMEM((8, LANES), jnp.float32),
+            pltpu.VMEM((CAP, BATCHES, 2 * row_count, 2 * LANES), jnp.bfloat16),
         ],
         compiler_params=pltpu.CompilerParams(vmem_limit_bytes=48 * 1024 * 1024),
         name="visibility",
-    )(live, place, *mine, *other)
+    )(owner_map, place, keep, turn, *mine, *other)
 
 
 def tiled_shards(volts, taps, owner_map, assign):
@@ -343,7 +450,6 @@
     inputs = volts.shape[1]
     spec_len = volts.shape[3] // NFFT - TAPS + 1
     my_row = lax.axis_index("row")
-    me = lax.axis_index("chan") * cols_count + lax.axis_index("col")
     total_inputs = 2 * STATIONS
     row_count = total_inputs // rows_count
     positions = jnp.arange(total_inputs, dtype=jnp.int32)
@@ -357,8 +463,6 @@
         jnp.where(row_of == my_row, 0, owners) + chan_of * cols_count + col_of
     ) * inputs + within
     place = (located[:, None] == positions[None, :]).astype(jnp.bfloat16)
-    owned = jnp.sum((owner_map == me).astype(jnp.int32))
-    live = jnp.stack([owned, my_row * row_count])
     mine = []
     other = []
     for batch in range(BATCHES):
@@ -368,14 +472,26 @@
         mine.append(flat)
         other.append(lax.ppermute(flat, "row", [(0, 1), (1, 0)]))
     scale = 1.0 / math.sqrt(2 * BATCHES * spec_len)
-    return visibility(scale, live, place, mine, other, row_count)
+    return visibility(scale, owner_map, place, mine, other, row_count)
+
+
+def fits(volts, owner_map, mesh):
+    rows = volts.shape[3] // NFFT
+    return (
+        4 * volts.shape[1] == LANES
+        and mesh.shape["row"] == 2
+        and rows - TAPS + 1 == 6 * UNIT
+        and -(-rows // BLOCK) % (2 * UNROLL) == UNROLL
+        and owner_map.shape[0] % 8 == 0
+        and TAPS * 2 * owner_map.shape[0] <= 384
+    )
 
 
 def solution(mesh):
     placed = (P(None, ("chan", "row", "col"), None, None), P(), P(), P())
 
     def shards(volts, taps, owner_map, assign):
-        if 4 * volts.shape[1] == LANES and mesh.shape["row"] == 2:
+        if fits(volts, owner_map, mesh):
             return tiled_shards(volts, taps, owner_map, assign)
         return general_shards(volts, taps, owner_map, assign)
 

time: 74.1 us -> 56.8 us (0.77)
  Pallas kernels: 42.1 us -> 26.9 us
  waiting for transfers between devices: 11.6 us -> 16.7 us
  starting transfers between devices: 15.3 us -> 12 us
  local copies, waits for them, and re-layouts: 2.57 us -> 0.32 us
  other arithmetic: 1.81 us -> 0.44 us
    pallas_call x2, Pallas kernels: 30.1 us -> 17.6 us  [spectra(): pl.pallas_call(functools.partial(spectra_kernel, batch, channels, owners,...]
    all_to_all x2, waiting for transfers between devices: 11.6 us -> 15.4 us  [tiled_shards(): lax.all_to_all(sent, ('chan', 'col'), split_axis=0, concat_axis=0, tiled=...]
    all_to_all x2, starting transfers between devices: 15.3 us -> 12 us  [tiled_shards(): lax.all_to_all(sent, ('chan', 'col'), split_axis=0, concat_axis=0, tiled=...]
    pallas_call x1, Pallas kernels: 11.9 us -> 9.37 us  [visibility(): pl.pallas_call(functools.partial(visibility_kernel, scale), out_shape=jax...]
    unnamed x14 -> x8, local copies, waits for them, and re-layouts: 2.28 us -> 0.03 us
    ppermute x2, waiting for transfers between devices: 0.01 us -> 1.26 us  [tiled_shards(): other.append(lax.ppermute(flat, 'row', [(0, 1), (1, 0)]))]
  transfers between devices with their start and end apart: 4 -> 4, of which waited for: 1 -> 3; matrix products, arithmetic and copies ran while one was open for 3% -> 1% of each run, Pallas kernels for 21% -> 16%
where the time goes in v2:
time: 56.8 us; the launch traced here: 56.5 us
  Pallas kernels  26.9 us (47%)
  waiting for transfers between devices  16.7 us (29%)
  starting transfers between devices  12 us (21%)
    pallas_call x2, Pallas kernels, spectra(): pl.pallas_call(functools.partial(spectra_kernel, batch, channels, owners,...  17.6 us
    all_to_all x2, waiting for transfers between devices, tiled_shards(): lax.all_to_all(sent, ('chan', 'col'), split_axis=0, concat_axis=0, tiled=...  15.4 us
    all_to_all x2, starting transfers between devices, tiled_shards(): lax.all_to_all(sent, ('chan', 'col'), split_axis=0, concat_axis=0, tiled=...  12 us
    pallas_call x1, Pallas kernels, visibility(): pl.pallas_call(functools.partial(visibility_kernel, scale), out_shape=jax...  9.37 us
    ppermute x2, waiting for transfers between devices, tiled_shards(): other.append(lax.ppermute(flat, 'row', [(0, 1), (1, 0)]))  1.26 us
  transfers between devices with their start and end apart: 4, of which 3 were waited for; matrix products, arithmetic and copies ran while one was open for 1% of the time, Pallas kernels for 16%

profile of v2, /device:TPU:0, one launch (start us, length us, event | category | flops | bytes accessed | tf_op | source)
XLA Modules:
  0.0 56.5 jit_solution(8439352989743537716)
XLA Ops:
  0.0 8.8 %spectra.2 = bf16[16,32,384]{2,1,0:T(8,128)(2,1)} custom-call(s32[24]{0:T(128)} %owner_ref.1, bf16[2,32,2,52736]{3,2,1,0:T(2,128)(2,1)} %volts_ref.3, f32[8,512]{1,0:T(8,128)} %taps_hbm.3, f32[48,512]{1,0:T(8,128)} %constant.82.clone.trig_hbm), custom_call_target="tpu_custom_call" | custom-call | flops 5184159744 | bytes 6750208 | tf_op jit(solution)/shard_map/spectra/pallas_call | solution.py:335
  8.8 8.4 %all-to-all-start = ((bf16[16,32,384]{2,1,0:T(8,128)(2,1)}), bf16[16,32,384]{2,1,0:T(8,128)(2,1)S(1)}, u32[]{:S(2)}, u32[]{:S(2)}) async-start(bf16[16,32,384]{2,1,0:T(8,128)(2,1)} %spectra.2), calls=%async_computation | async-start | bytes 786432 | tf_op jit(solution)/shard_map/all_to_all | solution.py:470
  17.1 0.0 copy-start.3
  17.1 0.0 copy-start
  17.2 0.0 copy-start.1
  17.2 0.0 copy-start.2
  17.2 8.8 %spectra.3 = bf16[16,32,384]{2,1,0:T(8,128)(2,1)} custom-call(s32[24]{0:T(128)} %owner_ref.1, bf16[2,32,2,52736]{3,2,1,0:T(2,128)(2,1)} %volts_ref.3, f32[8,512]{1,0:T(8,128)} %taps_hbm.3, f32[48,512]{1,0:T(8,128)} %constant.82.clone.trig_hbm), custom_call_target="tpu_custom_call" | custom-call | flops 5184159744 | bytes 6750208 | tf_op jit(solution)/shard_map/spectra/pallas_call | solution.py:335
  26.0 3.8 %all-to-all-done = bf16[16,32,384]{2,1,0:T(8,128)(2,1)S(1)} async-done(((bf16[16,32,384]{2,1,0:T(8,128)(2,1)}), bf16[16,32,384]{2,1,0:T(8,128)(2,1)S(1)}, u32[]{:S(2)}, u32[]{:S(2)}) %all-to-all-start) | async-done | bytes 393248 | tf_op jit(solution)/shard_map/all_to_all | solution.py:470
  29.8 3.6 %all-to-all-start.1 = ((bf16[16,32,384]{2,1,0:T(8,128)(2,1)}), bf16[16,32,384]{2,1,0:T(8,128)(2,1)S(1)}, u32[]{:S(2)}, u32[]{:S(2)}) async-start(bf16[16,32,384]{2,1,0:T(8,128)(2,1)} %spectra.3), calls=%async_computation.1 | async-start | bytes 786432 | tf_op jit(solution)/shard_map/all_to_all | solution.py:470
  33.4 0.0 copy-done.3
  33.4 0.1 broadcast_in_dim.11
  33.5 0.2 mul.27
  33.7 0.1 collective-permute-start
  33.8 11.6 %all-to-all-done.1 = bf16[16,32,384]{2,1,0:T(8,128)(2,1)S(1)} async-done(((bf16[16,32,384]{2,1,0:T(8,128)(2,1)}), bf16[16,32,384]{2,1,0:T(8,128)(2,1)S(1)}, u32[]{:S(2)}, u32[]{:S(2)}) %all-to-all-start.1) | async-done | bytes 393248 | tf_op jit(solution)/shard_map/all_to_all | solution.py:470
  45.4 0.0 collective-permute-start.1
  45.4 0.4 fusion.place_ref
  45.9 0.0 collective-permute-done.other_a
  45.9 1.3 %collective-permute-done.1.other_b = bf16[512,384]{1,0:T(8,128)(2,1)S(1)} collective-permute-done((bf16[512,384]{1,0:T(8,128)(2,1)S(1)}, bf16[512,384]{1,0:T(8,128)(2,1)S(1)}, u32[]{:S(2)}, u32[]{:S(2)}) %collective-permute-start.1) | collective-permute-done | bytes 393248 | tf_op jit(solution)/shard_map/ppermute | solution.py:473
  47.1 0.0 copy-done
  47.1 0.0 copy-done.1
  47.1 0.0 copy-done.2
  47.1 9.4 %visibility.1 = bf16[2,2,512,1024]{3,2,1,0:T(8,128)(2,1)} custom-call(s32[24]{0:T(128)S(1)} %copy-done.2, bf16[1024,1024]{1,0:T(8,128)(2,1)S(1)} %fusion.place_ref, bf16[2,16,256]{2,1,0:T(8,128)(2,1)S(1)} %copy-done.1, bf16[2,256,256]{2,1,0:T(8,128)(2,1)S(1)} %copy-done, bf16[512,384]{1,0:T(8,128)(2,1)S(1)} %bitcast.3, bf16[512,384]{1,0:T(8,128)(2,1)S(1)} %bitcast.5, ...), custom_call_target="tpu_custom_call" | custom-call | tf_op jit(solution)/shard_map/visibility/pallas_call | solution.py:429
  (2 shorter events, 0.0 us)
Async XLA Ops:
  8.8 21.0 %all-to-all-start = ((bf16[16,32,384]{2,1,0:T(8,128)(2,1)}), bf16[16,32,384]{2,1,0:T(8,128)(2,1)S(1)}, u32[]{:S(2)}, u32[]{:S(2)}) async-start(bf16[16,32,384]{2,1,0:T(8,128)(2,1)} %spectra.2), calls=%async_computation | async-start | bytes 786432 | tf_op jit(solution)/shard_map/all_to_all | solution.py:470
  17.1 16.2 %copy-start.3 = (s32[512]{0:T(512)S(1)}, s32[512]{0:T(512)}, u32[]{:S(2)}) copy-start(s32[512]{0:T(512)} %param.11) | copy-start | bytes 6148
  17.1 30.0 %copy-start = (bf16[2,256,256]{2,1,0:T(8,128)(2,1)S(1)}, bf16[2,256,256]{2,1,0:T(8,128)(2,1)}, u32[]{:S(2)}) copy-start(bf16[2,256,256]{2,1,0:T(8,128)(2,1)} %constant.84.clone.turn_ref) | copy-start | bytes 786436
  17.2 30.0 %copy-start.1 = (bf16[2,16,256]{2,1,0:T(8,128)(2,1)S(1)}, bf16[2,16,256]{2,1,0:T(8,128)(2,1)}, u32[]{:S(2)}) copy-start(bf16[2,16,256]{2,1,0:T(8,128)(2,1)} %constant.83.clone.keep_ref) | copy-start | bytes 49156
  17.2 30.0 %copy-start.2 = (s32[24]{0:T(128)S(1)}, s32[24]{0:T(128)}, u32[]{:S(2)}) copy-start(s32[24]{0:T(128)} %owner_ref.1) | copy-start | bytes 292
  29.8 15.6 %all-to-all-start.1 = ((bf16[16,32,384]{2,1,0:T(8,128)(2,1)}), bf16[16,32,384]{2,1,0:T(8,128)(2,1)S(1)}, u32[]{:S(2)}, u32[]{:S(2)}) async-start(bf16[16,32,384]{2,1,0:T(8,128)(2,1)} %spectra.3), calls=%async_computation.1 | async-start | bytes 786432 | tf_op jit(solution)/shard_map/all_to_all | solution.py:470
  33.7 12.2 %collective-permute-start = (bf16[512,384]{1,0:T(8,128)(2,1)S(1)}, bf16[512,384]{1,0:T(8,128)(2,1)S(1)}, u32[]{:S(2)}, u32[]{:S(2)}) collective-permute-start(bf16[512,384]{1,0:T(8,128)(2,1)S(1)} %bitcast.2), channel_id=1, source_target_pairs={{0,2},{2,0},{1,3},{3,1},{4,6},{6,4},{5,7},{7,5},{8,10},{10,8},{9,1... | collective-permute-start | bytes 1179656 | tf_op jit(solution)/shard_map/ppermute | solution.py:473
  45.4 1.7 %collective-permute-start.1 = (bf16[512,384]{1,0:T(8,128)(2,1)S(1)}, bf16[512,384]{1,0:T(8,128)(2,1)S(1)}, u32[]{:S(2)}, u32[]{:S(2)}) collective-permute-start(bf16[512,384]{1,0:T(8,128)(2,1)S(1)} %bitcast.4), channel_id=1, source_target_pairs={{0,2},{2,0},{1,3},{3,1},{4,6},{6,4},{5,7},{7,5},{8,10},{10,8},{9,1... | collective-permute-start | bytes 1179656 | tf_op jit(solution)/shard_map/ppermute | solution.py:473
